TPU v7x, 32 devices: a whole 2x2x4 slice. The times are simulated.
32 devices in a mesh: groups: 2 (over y), chan: 4 (over z), space: 2 (over x), pair: 2 (over core).
Axes of the slice: x: 2, y: 2, z: 4, core: 2. Of those that a mesh axis runs over, the one named last changes fastest.
Arguments:
- grad_out: bfloat16 [512, 32, 1024], P('chan', ('groups', 'space', 'pair')), parts along dimension 1, may hold values from -6 to 6
- conv_weight: bfloat16 [27, 512, 512], P(None, 'chan'), may hold values from -0.0546875 to 0.0546875
- pre_act: bfloat16 [32, 1024, 512], P(('groups', 'space', 'pair'), 'chan'), parts along dimension 0, may hold values from -6 to 6
- down_weight: bfloat16 [8, 256, 512], replicated, may hold values from -0.25 to 0.25
Outputs:
- grad_fine: bfloat16 [32, 1024, 8, 256], P(('groups', 'space', 'pair'), 'chan'), parts along dimension 0
There are 2 independent parts, one for each index of `groups`. A program takes and returns all parts, laid end to end along the dimension named above; an argument that names none is the same for every part. Nothing has to cross between parts.
All inputs are finite; a program needn't handle non-finite values.
Results may differ from a plain program's by a relative error of at most 0.025.
Values may be sent and summed in bfloat16 or wider, within the bound.
No kernel may reach another device: no remote copies, remote signals or barrier semaphores. Data moves between devices by JAX's collectives and lax.ppermute only.
A program may use at most 64 MiB of HBM per device.

v0:
```python
import math
import jax
import jax.numpy as jnp
from jax import lax
from jax.sharding import PartitionSpec as P

NZ = 8


def with_halo(cells, sides, width):
    for axis, dim in sides:
        count = lax.axis_size(axis)
        ends = count - 1
        head = lax.slice_in_dim(cells, 0, width, axis=dim)
        tail = lax.slice_in_dim(cells, cells.shape[dim] - width, cells.shape[dim], axis=dim)
        cells = jnp.concatenate(
            [
                lax.ppermute(tail, axis, [(i, (i + 1) % count) for i in range(ends)]),
                cells,
                lax.ppermute(head, axis, [((i + 1) % count, i) for i in range(ends)]),
            ],
            axis=dim,
        )
    return cells


def shifted_stack(padded, depth):
    extent = padded.shape[1] - 2
    plane_len = padded.shape[2]
    widened = jnp.pad(padded, ((0, 0), (0, 0), (depth + 1, depth + 1)))
    z_index = jnp.arange(plane_len, dtype=jnp.int32) % depth
    pieces = []
    for step_x in (-1, 0, 1):
        x_rows = widened[:, 1 - step_x : 1 - step_x + extent, :]
        for step_y in (-1, 0, 1):
            for step_z in (-1, 0, 1):
                offset = step_y * depth + step_z
                piece = x_rows[:, :, depth + 1 - offset : depth + 1 - offset + plane_len]
                inside = (z_index - step_z >= 0) & (z_index - step_z < depth)
                pieces.append(jnp.where(inside, piece, jnp.zeros_like(piece)))
    return jnp.stack(pieces)


def gelu_slope(values):
    return 0.5 * (1.0 + jax.scipy.special.erf(values / math.sqrt(2.0))) + values * jnp.exp(
        -0.5 * values * values
    ) / math.sqrt(2.0 * math.pi)


def body(grad_out, conv_weight, pre_act, down_weight):
    padded = with_halo(grad_out, ((("space", "pair"), 1),), 1)
    stacked = shifted_stack(padded, NZ)
    partial_sum = lax.dot_general(
        stacked, conv_weight, (((0, 1), (0, 1)), ((), ())), preferred_element_type=jnp.float32
    )
    owned = lax.psum_scatter(
        partial_sum.astype(jnp.bfloat16), "chan", scatter_dimension=2, tiled=True
    )
    grad_act = lax.all_to_all(owned, "chan", split_axis=1, concat_axis=2, tiled=True)
    values = pre_act.astype(jnp.float32)
    grad_pre = (grad_act.astype(jnp.float32) * gelu_slope(values)).astype(jnp.bfloat16)
    result = lax.dot_general(
        grad_pre, down_weight, (((2,), (2,)), ((), ())), preferred_element_type=jnp.float32
    )
    return result.astype(jnp.bfloat16)


def solution(mesh):
    in_specs = (
        P("chan", ("groups", "space", "pair"), None),
        P(None, "chan", None),
        P(("groups", "space", "pair"), "chan", None),
        P(),
    )
    out_specs = P(("groups", "space", "pair"), "chan", None, None)
    return jax.shard_map(body, mesh=mesh, in_specs=in_specs, out_specs=out_specs, check_vma=False)
```

profile of v0, /device:TPU:0, one launch (start us, length us, event | category | flops | bytes accessed | tf_op | source)
XLA Modules:
  0.0 204.0 jit_solution(13061538225299000226)
XLA Ops:
  6.5 0.0 reduce-scatter.4.cloned.1.call-start
  6.5 2.8 %copy.39 = bf16[128,4,1024]{0,2,1:T(8,128)(2,1)} copy(bf16[128,4,1024]{2,1,0:T(4,128)(2,1)} %param.4) | data formatting | bytes 2097152 | tf_op args[0]
  9.3 1.2 fusion.98
  10.5 2.4 %collective-permute-start = (bf16[128,1,1024]{0,2,1:T(8,128)(2,1)S(1)}, bf16[128,1,1024]{0,2,1:T(8,128)(2,1)S(1)}, u32[]{:S(2)}, u32[]{:S(2)}) collective-permute-start(bf16[128,1,1024]{0,2,1:T(8,128)(2,1)S(1)} %get-tuple-element.5), channel_id=1, source_target_pairs={{0,1},{1,2},{2,3},{4,5},{5,6},{6,7},{8,9},{9,10},{10,11},{12,13},{... | collective-permute-start | bytes 786440 | tf_op jit(solution)/shard_map/ppermute | solution.py:18
  12.9 1.3 collective-permute-start.1
  14.2 0.0 collective-permute-done
  14.2 4.2 %collective-permute-done.1 = bf16[128,1,1024]{0,2,1:T(8,128)(2,1)S(1)} collective-permute-done((bf16[128,1,1024]{0,2,1:T(8,128)(2,1)S(1)}, bf16[128,1,1024]{0,2,1:T(8,128)(2,1)S(1)}, u32[]{:S(2)}, u32[]{:S(2)}) %collective-permute-start.1) | collective-permute-done | bytes 262176 | tf_op jit(solution)/shard_map/ppermute | solution.py:20
  18.4 1.6 fusion.18
  20.0 0.4 fusion.72
  20.4 0.6 fusion.70
  21.0 0.5 fusion.68
  21.5 0.6 fusion.66
  22.1 0.5 fusion.64
  22.6 0.5 fusion.61
  23.1 0.6 fusion.59
  23.7 0.6 fusion.57
  24.3 0.5 fusion.55
  24.8 0.6 fusion.53
  25.4 0.6 fusion.51
  26.0 0.5 fusion.49
  26.5 0.6 fusion.47
  27.1 0.5 bitcast_dynamic-update-slice_fusion
  27.6 0.5 fusion.45
  28.1 0.6 fusion.43
  28.7 0.6 fusion.41
  29.3 0.5 fusion.39
  29.8 0.6 fusion.37
  30.4 0.6 fusion.35
  31.0 0.5 fusion.33
  31.5 0.6 fusion.31
  32.1 0.5 fusion.29
  32.6 0.5 fusion.26
  33.1 0.8 fusion.24
  33.9 0.6 fusion.22
  34.5 0.5 fusion.20
  35.0 17.0 %bitcast_convert_fusion = bf16[4,1024,512]{2,1,0:T(8,128)(2,1)} fusion(bf16[27,128,4,1024]{1,3,0,2:T(8,128)(2,1)S(1)} %fusion.20, bf16[27,128,512]{2,1,0:T(8,128)(2,1)S(1)} %copy-done), kind=kOutput, calls=%fused_computation | convolution fusion | flops 14497611776 | bytes 36044800 | tf_op jit(solution)/shard_map/dot_general | solution.py:53
  52.0 8.0 %copy.76 = bf16[4,1024,512]{1,0,2:T(4,128)(2,1)} copy(bf16[4,1024,512]{2,1,0:T(8,128)(2,1)} %bitcast_convert_fusion) | data formatting | bytes 8388608
  60.0 6.5 %copy.79 = bf16[64,8,4,1024]{3,1,2,0:T(8,128)(2,1)} copy(bf16[64,8,4,1024]{3,2,1,0:T(4,128)(2,1)} %bitcast.184) | data formatting | bytes 8388608
  66.5 0.0 reduce-scatter.4.cloned.1.call-update
  66.5 81.7 %reduce-scatter.4.cloned.1.call-done = bf16[128,4096]{1,0:T(8,128)(2,1)} async-done(((bf16[512,4096]{1,0:T(8,128)(2,1)}), bf16[128,4096]{1,0:T(8,128)(2,1)}) %reduce-scatter.4.cloned.1.call-update) | async-done | bytes 1048592
  148.2 1.8 reshape.11
  150.0 1.5 copy.71
  151.5 29.8 %all_to_all.4 = bf16[4,1024,128]{2,0,1:T(4,128)(2,1)S(1)} all-to-all(bf16[4,1024,128]{2,0,1:T(4,128)(2,1)S(1)} %copy.71), channel_id=1, replica_groups=mesh['groups'=2,'chan'=4,'space'=2,'pair'=2] {'chan'}, dimensions={1} | all-to-all | bytes 2097152 | tf_op jit(solution)/shard_map/all_to_all | solution.py:59
  181.3 0.1 convert_bitcast_fusion
  181.4 2.7 %copy.72 = f32[4,256,4,128]{3,2,1,0:T(4,128)} copy(f32[4,256,4,128]{3,0,1,2:T(4,128)S(1)} %convert_bitcast_fusion) | data formatting | bytes 4194304 | tf_op jit(solution)/shard_map/convert_element_type | solution.py:61
  184.1 3.3 %reshape.4 = f32[4,256,512]{2,1,0:T(8,128)} reshape(f32[4,256,4,128]{3,2,1,0:T(4,128)} %copy.72) | data formatting | bytes 4194304 | tf_op jit(solution)/shard_map/convert_element_type | solution.py:61
  187.4 5.3 %convolution_convert_fusion = bf16[4,256,8,256]{3,1,2,0:T(8,128)(2,1)S(1)} fusion(bf16[8,256,512]{2,1,0:T(8,128)(2,1)} %param.7, f32[4,256,512]{2,1,0:T(8,128)} %reshape.4, bf16[4,256,512]{2,1,0:T(8,128)(2,1)} %param.6), kind=kOutput, calls=%fused_computation.10 | convolution fusion | flops 2155347968 | bytes 9437184 | tf_op jit(solution)/shard_map/dot_general | solution.py:62
  192.7 4.5 %copy.73 = bf16[4,256,8,256]{3,2,1,0:T(8,128)(2,1)} copy(bf16[4,256,8,256]{3,1,2,0:T(8,128)(2,1)S(1)} %convolution_convert_fusion) | data formatting | bytes 8388608 | tf_op jit(solution)/shard_map/convert_element_type | solution.py:65
  (9 shorter events, 0.0 us)
Async XLA Ops:
  6.5 28.4 %copy-start = (bf16[27,128,512]{2,1,0:T(8,128)(2,1)S(1)}, bf16[27,128,512]{2,1,0:T(8,128)(2,1)}, u32[]{:S(2)}) copy-start(bf16[27,128,512]{2,1,0:T(8,128)(2,1)} %param.5) | copy-start | bytes 10616836
  6.5 141.6 %reduce-scatter.4.cloned.1.call-start = ((), (), s32[]{:S(2)}) async-start(), calls=%async_computation.2 | async-start | bytes 5242880
  9.3 12.8 %copy-start.2 = (bf16[128,4,1024]{0,2,1:T(8,128)(2,1)S(1)}, bf16[128,4,1024]{0,2,1:T(8,128)(2,1)}, u32[]{:S(2)}) copy-start(bf16[128,4,1024]{0,2,1:T(8,128)(2,1)} %copy.39) | copy-start | bytes 3145732
  10.5 3.7 %collective-permute-start = (bf16[128,1,1024]{0,2,1:T(8,128)(2,1)S(1)}, bf16[128,1,1024]{0,2,1:T(8,128)(2,1)S(1)}, u32[]{:S(2)}, u32[]{:S(2)}) collective-permute-start(bf16[128,1,1024]{0,2,1:T(8,128)(2,1)S(1)} %get-tuple-element.5), channel_id=1, source_target_pairs={{0,1},{1,2},{2,3},{4,5},{5,6},{6,7},{8,9},{9,10},{10,11},{12,13},{... | collective-permute-start | bytes 786440 | tf_op jit(solution)/shard_map/ppermute | solution.py:18
  12.9 5.5 %collective-permute-start.1 = (bf16[128,1,1024]{0,2,1:T(8,128)(2,1)S(1)}, bf16[128,1,1024]{0,2,1:T(8,128)(2,1)S(1)}, u32[]{:S(2)}, u32[]{:S(2)}) collective-permute-start(bf16[128,1,1024]{0,2,1:T(8,128)(2,1)S(1)} %get-tuple-element.6), channel_id=1, source_target_pairs={{1,0},{2,1},{3,2},{5,4},{6,5},{7,6},{9,8},{10,9},{11,10},{13,12},{... | collective-permute-start | bytes 786440 | tf_op jit(solution)/shard_map/ppermute | solution.py:20
  184.1 13.1 %copy-start.1 = (bf16[27,128,512]{2,1,0:T(8,128)(2,1)S(1)}, bf16[27,128,512]{2,1,0:T(8,128)(2,1)}, u32[]{:S(2)}) copy-start(bf16[27,128,512]{2,1,0:T(8,128)(2,1)} %param.5) | copy-start | bytes 10616836
Sparse Core Ops, SparseCore 0:
  66.6 81.4 reduce-scatter.3
where the time goes:
time: 204 us
  waiting for transfers between devices  85.8 us (42%)
  local copies, waits for them, and re-layouts  32.2 us (16%)
  blocking collectives  29.8 us (15%)
  matrix products  22.4 us (11%)
  other arithmetic  16.5 us (8%)
  between operations  13.7 us (7%)
  starting transfers between devices  3.67 us (2%)
    unnamed x2, waiting for transfers between devices  81.7 us
    all_to_all x1, blocking collectives, body(): lax.all_to_all(owned, 'chan', split_axis=1, concat_axis=2, tiled=True)  29.8 us
    unnamed x10, local copies, waits for them, and re-layouts  19.1 us
    dot_general x1, matrix products, body(): lax.dot_general(stacked, conv_weight, (((0, 1), (0, 1)), ((), ())), prefe...  17 us
    unnamed x26, other arithmetic  14.2 us
    convert_element_type x2, local copies, waits for them, and re-layouts, body(): grad_act.astype(jnp.float32) * gelu_slope(values)  5.93 us
    dot_general x1, matrix products, body(): lax.dot_general(grad_pre, down_weight, (((2,), (2,)), ((), ())), preferre...  5.33 us
    convert_element_type x1, local copies, waits for them, and re-layouts, body(): return result.astype(jnp.bfloat16)  4.47 us
  transfers between devices with their start and end apart: 3, of which 2 were waited for; matrix products, arithmetic and copies ran while one was open for 0% of the time, Pallas kernels for 0%

commit v1 on v0

--- a/solution.py
+++ b/solution.py
@@ -1,10 +1,48 @@
+import functools
 import math
 import jax
 import jax.numpy as jnp
 from jax import lax
 from jax.sharding import PartitionSpec as P
+from jax.lax import axis_index, ppermute, psum
 
 NZ = 8
+
+
+def manage_steps_all_now(local, which_dim, buf):
+    d_next, heard = (local.shape[:which_dim], local.shape[which_dim + 1 :])
+    now = local.reshape(*d_next, buf, -1, *heard)
+    extra = jnp.moveaxis(now, which_dim, 0)
+    return extra
+
+
+def plan_joints(vec, array_axis):
+    vec = jnp.moveaxis(vec, 0, array_axis)
+    value_now = vec.shape
+    y1 = vec.reshape(
+        *value_now[:array_axis],
+        value_now[array_axis] * value_now[array_axis + 1],
+        *value_now[array_axis + 2 :]
+    )
+    return y1
+
+
+def link_inputs_all(z, mesh_dim, packet, xx):
+    next_value = psum(1, axis_name=mesh_dim)
+    parts_out = axis_index(mesh_dim)
+    r_now, v_next = (next_value, parts_out)
+    opened = manage_steps_all_now(z, packet, r_now)
+    samples = [opened[v_next]]
+    for u in [*range(1, r_now)]:
+        tile_out = opened[v_next ^ u]
+        block_next = ppermute(tile_out, axis_name=mesh_dim, perm=[(b, b ^ u) for b in range(r_now)])
+        samples.append(block_next)
+    opened = jnp.stack(samples, axis=0)[v_next ^ jnp.arange(r_now)]
+    answer = plan_joints(opened, xx)
+    return answer
+
+
+direct_local_data = functools.partial(link_inputs_all, mesh_dim="chan", packet=1, xx=2)
 
 
 def with_halo(cells, sides, width):
@@ -56,7 +94,7 @@
     owned = lax.psum_scatter(
         partial_sum.astype(jnp.bfloat16), "chan", scatter_dimension=2, tiled=True
     )
-    grad_act = lax.all_to_all(owned, "chan", split_axis=1, concat_axis=2, tiled=True)
+    grad_act = direct_local_data(owned)
     values = pre_act.astype(jnp.float32)
     grad_pre = (grad_act.astype(jnp.float32) * gelu_slope(values)).astype(jnp.bfloat16)
     result = lax.dot_general(

time: 204 us -> 199 us (0.975); the launches traced: 204 us -> 197 us
  blocking collectives: 29.8 us -> 0 us
  waiting for transfers between devices: 85.8 us -> 103 us
  starting transfers between devices: 3.67 us -> 8.12 us
  other arithmetic: 16.5 us -> 20.5 us
    all_to_all x1 -> x0, blocking collectives: 29.8 us -> none  [body(): lax.all_to_all(owned, 'chan', split_axis=1, concat_axis=2, tiled=True)]
    ppermute x0 -> x3, waiting for transfers between devices: none -> 17.2 us  [link_inputs_all(): ppermute(tile_out, axis_name=mesh_dim, perm=[(b, b ^ u) for b in range(r_...]
    ppermute x0 -> x3, starting transfers between devices: none -> 4.46 us  [link_inputs_all(): ppermute(tile_out, axis_name=mesh_dim, perm=[(b, b ^ u) for b in range(r_...]
    convert_element_type x2 -> x1, local copies, waits for them, and re-layouts: 5.93 us -> 1.81 us  [body(): grad_act.astype(jnp.float32) * gelu_slope(values)]
    unnamed x10 -> x18, local copies, waits for them, and re-layouts: 19.1 us -> 22.3 us
    convert_element_type x0 -> x1, other arithmetic: none -> 2.71 us  [body(): (grad_act.astype(jnp.float32) * gelu_slope(values)).astype(jnp.bfloat16)]
  transfers between devices with their start and end apart: 3 -> 6, of which waited for: 2 -> 4; matrix products, arithmetic and copies ran while one was open for 0% -> 1% of each run, Pallas kernels for 0% -> 0%
where the time goes in v1:
time: 199 us; the launch traced here: 197 us
  waiting for transfers between devices  103 us (52%)
  local copies, waits for them, and re-layouts  30.6 us (15%)
  matrix products  21 us (11%)
  other arithmetic  20.5 us (10%)
  between operations  13.7 us (7%)
  starting transfers between devices  8.12 us (4%)
    unnamed x2, waiting for transfers between devices  81.6 us
    unnamed x18, local copies, waits for them, and re-layouts  22.3 us
    ppermute x3, waiting for transfers between devices, link_inputs_all(): ppermute(tile_out, axis_name=mesh_dim, perm=[(b, b ^ u) for b in range(r_...  17.2 us
    dot_general x1, matrix products, body(): lax.dot_general(stacked, conv_weight, (((0, 1), (0, 1)), ((), ())), prefe...  17 us
    unnamed x26, other arithmetic  14.2 us
    convert_element_type x1, local copies, waits for them, and re-layouts, body(): return result.astype(jnp.bfloat16)  4.47 us
    ppermute x3, starting transfers between devices, link_inputs_all(): ppermute(tile_out, axis_name=mesh_dim, perm=[(b, b ^ u) for b in range(r_...  4.46 us
    ppermute x1, waiting for transfers between devices, with_halo(): lax.ppermute(head, axis, [((i + 1) % count, i) for i in range(ends)])  4.17 us
  transfers between devices with their start and end apart: 6, of which 4 were waited for; matrix products, arithmetic and copies ran while one was open for 1% of the time, Pallas kernels for 0%

profile of v1, /device:TPU:0, one launch (start us, length us, event | category | flops | bytes accessed | tf_op | source)
XLA Modules:
  0.0 196.9 jit_solution(10058135268933550500)
XLA Ops:
  6.5 2.8 %copy.107 = bf16[128,4,1024]{0,2,1:T(8,128)(2,1)} copy(bf16[128,4,1024]{2,1,0:T(4,128)(2,1)} %param.4) | data formatting | bytes 2097152 | tf_op args[0]
  9.3 1.2 fusion.89
  10.5 2.4 %collective-permute-start = (bf16[128,1,1024]{0,2,1:T(8,128)(2,1)S(1)}, bf16[128,1,1024]{0,2,1:T(8,128)(2,1)S(1)}, u32[]{:S(2)}, u32[]{:S(2)}) collective-permute-start(bf16[128,1,1024]{0,2,1:T(8,128)(2,1)S(1)} %get-tuple-element.9), channel_id=1, source_target_pairs={{0,1},{1,2},{2,3},{4,5},{5,6},{6,7},{8,9},{9,10},{10,11},{12,13},{... | collective-permute-start | bytes 786440 | tf_op jit(solution)/shard_map/ppermute | solution.py:56
  12.9 1.3 collective-permute-start.1
  14.2 4.2 %collective-permute-done.1 = bf16[128,1,1024]{0,2,1:T(8,128)(2,1)S(1)} collective-permute-done((bf16[128,1,1024]{0,2,1:T(8,128)(2,1)S(1)}, bf16[128,1,1024]{0,2,1:T(8,128)(2,1)S(1)}, u32[]{:S(2)}, u32[]{:S(2)}) %collective-permute-start.1) | collective-permute-done | bytes 262176 | tf_op jit(solution)/shard_map/ppermute | solution.py:58
  18.4 1.6 fusion.18
  20.4 0.6 fusion.70
  21.5 0.6 fusion.66
  22.1 0.5 fusion.64
  22.6 0.5 fusion.61
  23.1 0.6 fusion.59
  23.7 0.6 fusion.57
  24.3 0.5 fusion.55
  24.8 0.6 fusion.53
  25.4 0.6 fusion.51
  26.0 0.5 fusion.49
  26.5 0.6 fusion.47
  27.1 0.5 bitcast_dynamic-update-slice_fusion
  27.6 0.5 fusion.45
  28.1 0.6 fusion.43
  28.7 0.6 fusion.41
  29.3 0.5 fusion.39
  29.8 0.6 fusion.37
  30.4 0.6 fusion.35
  31.0 0.5 fusion.33
  31.5 0.6 fusion.31
  32.1 0.5 fusion.29
  33.1 0.8 fusion.24
  33.9 0.6 fusion.22
  35.0 17.0 %bitcast_convert_fusion = bf16[4,1024,512]{2,1,0:T(8,128)(2,1)} fusion(bf16[27,128,4,1024]{1,3,0,2:T(8,128)(2,1)S(1)} %fusion.20, bf16[27,128,512]{2,1,0:T(8,128)(2,1)S(1)} %copy-done), kind=kOutput, calls=%fused_computation.1 | convolution fusion | flops 14497611776 | bytes 36044800 | tf_op jit(solution)/shard_map/dot_general | solution.py:91
  52.0 8.0 %copy.151 = bf16[4,1024,512]{1,0,2:T(4,128)(2,1)} copy(bf16[4,1024,512]{2,1,0:T(8,128)(2,1)} %bitcast_convert_fusion) | data formatting | bytes 8388608
  60.0 6.6 %copy.157 = bf16[64,8,4,1024]{3,1,2,0:T(8,128)(2,1)} copy(bf16[64,8,4,1024]{3,2,1,0:T(4,128)(2,1)} %bitcast.208) | data formatting | bytes 8388608
  66.6 81.6 %reduce-scatter.4.cloned.1.call-done = bf16[128,4096]{1,0:T(8,128)(2,1)} async-done(((bf16[512,4096]{1,0:T(8,128)(2,1)}), bf16[128,4096]{1,0:T(8,128)(2,1)}) %reduce-scatter.4.cloned.1.call-update) | async-done | bytes 1048592
  148.2 1.8 reshape.44
  150.1 1.0 copy.152
  151.2 1.6 collective-permute-start.2
  152.8 1.6 collective-permute-start.3
  154.4 1.3 collective-permute-start.4
  155.7 1.3 copy.144
  157.0 7.5 %collective-permute-done.2 = bf16[4,256,128]{2,1,0:T(8,128)(2,1)S(1)} collective-permute-done((bf16[4,256,128]{2,1,0:T(8,128)(2,1)S(1)}, bf16[4,256,128]{2,1,0:T(8,128)(2,1)S(1)}, u32[]{:S(2)}, u32[]{:S(2)}) %collective-permute-start.2) | collective-permute-done | bytes 262176 | tf_op jit(solution)/shard_map/ppermute | solution.py:38
  164.4 9.7 %collective-permute-done.3 = bf16[4,256,128]{2,1,0:T(8,128)(2,1)S(1)} collective-permute-done((bf16[4,256,128]{2,1,0:T(8,128)(2,1)S(1)}, bf16[4,256,128]{2,1,0:T(8,128)(2,1)S(1)}, u32[]{:S(2)}, u32[]{:S(2)}) %collective-permute-start.3) | collective-permute-done | bytes 262176 | tf_op jit(solution)/shard_map/ppermute | solution.py:38
  174.1 0.7 copy-done.4
  174.9 1.2 pad_maximum_fusion.2
  176.1 0.7 gather_fusion
  177.0 1.8 copy.143
  178.9 2.7 %fusion.13 = bf16[4,256,512]{1,2,0:T(8,128)(2,1)S(1)} fusion(bf16[4,256,512]{1,2,0:T(8,128)(2,1)} %copy.144, f32[4,256,4,128]{1,3,2,0:T(8,128)} %copy.143), kind=kLoop, calls=%fused_computation.21 | loop fusion | flops 5767168 | bytes 4194304 | tf_op jit(solution)/shard_map/convert_element_type | solution.py:99
  181.6 4.0 %convolution_convert_fusion = bf16[4,256,8,256]{3,1,2,0:T(8,128)(2,1)S(1)} fusion(bf16[8,256,512]{2,1,0:T(8,128)(2,1)} %param.7, bf16[4,256,512]{1,2,0:T(8,128)(2,1)S(1)} %fusion.13), kind=kOutput, calls=%fused_computation.11 | convolution fusion | flops 2149580800 | bytes 7340032 | tf_op jit(solution)/shard_map/dot_general | solution.py:100
  185.6 4.5 %copy.146 = bf16[4,256,8,256]{3,2,1,0:T(8,128)(2,1)} copy(bf16[4,256,8,256]{3,1,2,0:T(8,128)(2,1)S(1)} %convolution_convert_fusion) | data formatting | bytes 8388608 | tf_op jit(solution)/shard_map/convert_element_type | solution.py:103
  (26 shorter events, 2.3 us)
Async XLA Ops:
  6.5 28.4 %copy-start = (bf16[27,128,512]{2,1,0:T(8,128)(2,1)S(1)}, bf16[27,128,512]{2,1,0:T(8,128)(2,1)}, u32[]{:S(2)}) copy-start(bf16[27,128,512]{2,1,0:T(8,128)(2,1)} %param.5) | copy-start | bytes 10616836
  6.5 141.7 %reduce-scatter.4.cloned.1.call-start = ((), (), s32[]{:S(2)}) async-start(), calls=%async_computation.1 | async-start | bytes 5242880
  9.3 12.8 %copy-start.2 = (bf16[128,4,1024]{0,2,1:T(8,128)(2,1)S(1)}, bf16[128,4,1024]{0,2,1:T(8,128)(2,1)}, u32[]{:S(2)}) copy-start(bf16[128,4,1024]{0,2,1:T(8,128)(2,1)} %copy.107) | copy-start | bytes 3145732
  10.5 3.7 %collective-permute-start = (bf16[128,1,1024]{0,2,1:T(8,128)(2,1)S(1)}, bf16[128,1,1024]{0,2,1:T(8,128)(2,1)S(1)}, u32[]{:S(2)}, u32[]{:S(2)}) collective-permute-start(bf16[128,1,1024]{0,2,1:T(8,128)(2,1)S(1)} %get-tuple-element.9), channel_id=1, source_target_pairs={{0,1},{1,2},{2,3},{4,5},{5,6},{6,7},{8,9},{9,10},{10,11},{12,13},{... | collective-permute-start | bytes 786440 | tf_op jit(solution)/shard_map/ppermute | solution.py:56
  12.9 5.5 %collective-permute-start.1 = (bf16[128,1,1024]{0,2,1:T(8,128)(2,1)S(1)}, bf16[128,1,1024]{0,2,1:T(8,128)(2,1)S(1)}, u32[]{:S(2)}, u32[]{:S(2)}) collective-permute-start(bf16[128,1,1024]{0,2,1:T(8,128)(2,1)S(1)} %get-tuple-element.10), channel_id=1, source_target_pairs={{1,0},{2,1},{3,2},{5,4},{6,5},{7,6},{9,8},{10,9},{11,10},{13,12},{... | collective-permute-start | bytes 786440 | tf_op jit(solution)/shard_map/ppermute | solution.py:58
  60.0 95.7 %copy-start.3 = (bf16[4,256,512]{2,1,0:T(8,128)(2,1)S(1)}, bf16[4,256,512]{2,1,0:T(8,128)(2,1)}, u32[]{:S(2)}) copy-start(bf16[4,256,512]{2,1,0:T(8,128)(2,1)} %param.6) | copy-start | bytes 3145732
  151.2 13.2 %collective-permute-start.2 = (bf16[4,256,128]{2,1,0:T(8,128)(2,1)S(1)}, bf16[4,256,128]{2,1,0:T(8,128)(2,1)S(1)}, u32[]{:S(2)}, u32[]{:S(2)}) collective-permute-start(bf16[4,256,128]{2,1,0:T(8,128)(2,1)S(1)} %get-tuple-element.7), channel_id=1, source_target_pairs={{0,4},{4,0},{8,12},{12,8},{1,5},{5,1},{9,13},{13,9},{2,6},{6,2},{1... | collective-permute-start | bytes 786440 | tf_op jit(solution)/shard_map/ppermute | solution.py:38
  152.8 21.4 %collective-permute-start.3 = (bf16[4,256,128]{2,1,0:T(8,128)(2,1)S(1)}, bf16[4,256,128]{2,1,0:T(8,128)(2,1)S(1)}, u32[]{:S(2)}, u32[]{:S(2)}) collective-permute-start(bf16[4,256,128]{2,1,0:T(8,128)(2,1)S(1)} %get-tuple-element.6), channel_id=1, source_target_pairs={{0,8},{4,12},{8,0},{12,4},{1,9},{5,13},{9,1},{13,5},{2,10},{6,14},... | collective-permute-start | bytes 786440 | tf_op jit(solution)/shard_map/ppermute | solution.py:38
  154.4 19.7 %collective-permute-start.4 = (bf16[4,256,128]{2,1,0:T(8,128)(2,1)S(1)}, bf16[4,256,128]{2,1,0:T(8,128)(2,1)S(1)}, u32[]{:S(2)}, u32[]{:S(2)}) collective-permute-start(bf16[4,256,128]{2,1,0:T(8,128)(2,1)S(1)} %get-tuple-element.8), channel_id=1, source_target_pairs={{0,12},{4,8},{8,4},{12,0},{1,13},{5,9},{9,5},{13,1},{2,14},{6,10},... | collective-permute-start | bytes 786440 | tf_op jit(solution)/shard_map/ppermute | solution.py:38
  174.1 0.7 copy-start.4
  174.1 0.8 copy-start.5
  178.9 11.2 %copy-start.1 = (bf16[27,128,512]{2,1,0:T(8,128)(2,1)S(1)}, bf16[27,128,512]{2,1,0:T(8,128)(2,1)}, u32[]{:S(2)}) copy-start(bf16[27,128,512]{2,1,0:T(8,128)(2,1)} %param.5) | copy-start | bytes 10616836
Sparse Core Ops, SparseCore 0:
  66.7 81.4 reduce-scatter.3
